TPU v7x, 32 devices: a whole 2x2x4 slice. The times are simulated.
32 devices in a mesh: dp: 16 (over z, y, x), tensor: 2 (over core).
Axes of the slice: x: 2, y: 2, z: 4, core: 2. Of those that a mesh axis runs over, the one named last changes fastest.
Arguments:
- normed: bfloat16 [3072, 8192], P('dp', 'tensor'), may hold values from -6 to 6
- stored_queries: bfloat16 [3072, 4096], P('dp', 'tensor'), may hold values from -170 to 170
- stored_keys: bfloat16 [3072, 1024], P('dp', 'tensor'), may hold values from -7 to 7
- stored_values: bfloat16 [3072, 1024], P('dp', 'tensor'), may hold values from -6 to 6
- head_output_grad: bfloat16 [3072, 4096], P('dp', 'tensor'), may hold values from -6 to 6
- document_index: int32 [16, 192], P('dp'), may hold values from 0 to 7, never falling along the last dimension, each value on 1 to 72 neighbouring positions
- query_projection_weight: bfloat16 [8192, 4096], P('dp', 'tensor'), may hold values from -0.0625 to 0.0625
- key_projection_weight: bfloat16 [8192, 1024], P('dp', 'tensor'), may hold values from -0.0625 to 0.0625
- value_projection_weight: bfloat16 [8192, 1024], P('dp', 'tensor'), may hold values from -0.0625 to 0.0625
- adapter_down_maps: bfloat16 [8192, 192], P('tensor'), may hold values from -0.0625 to 0.0625
- query_up_map: bfloat16 [64, 4096], P(None, 'tensor'), may hold values from -0.75 to 0.75
- key_value_up_maps: bfloat16 [2, 64, 1024], P(None, None, 'tensor'), may hold values from -0.75 to 0.75
Outputs:
- normed_input_grad: bfloat16 [3072, 8192], P('dp', 'tensor')
- down_grad: float32 [8192, 192], P('tensor')
- query_up_grad: float32 [64, 4096], P(None, 'tensor')
- key_value_up_grad: float32 [2, 64, 1024], P(None, None, 'tensor')
All inputs are finite; a program needn't handle non-finite values.
Results may differ from a plain program's by a relative error of at most 0.0095.
Values may be sent and summed in bfloat16 or wider, within the bound.
No kernel may reach another device: no remote copies, remote signals or barrier semaphores. Data moves between devices by JAX's collectives and lax.ppermute only.
A program may use at most 192 MiB of HBM per device.

v0:
```python
import math
import jax
import jax.numpy as jnp
from jax import lax
from jax.sharding import PartitionSpec as P

QUERY_HEADS = 32
KEY_HEADS = 8
HEAD_SIZE = 128
ADAPTER_RANK = 64
adapter_scale = 0.5


def attention_backward(queries, keyrows, value_row_block, output_gradient, ids):
    token_count = queries.shape[0]
    key_value_heads = keyrows.shape[1] // HEAD_SIZE
    query_group = QUERY_HEADS // KEY_HEADS
    scale = 1.0 / math.sqrt(HEAD_SIZE)
    qmat = queries.reshape(token_count, key_value_heads, query_group, HEAD_SIZE)
    kmat = keyrows.reshape(token_count, key_value_heads, HEAD_SIZE)
    value_matrix = value_row_block.reshape(token_count, key_value_heads, HEAD_SIZE)
    output_matrix = output_gradient.reshape(token_count, key_value_heads, query_group, HEAD_SIZE)
    same = ids[:, None] == ids[None, :]
    scores = jnp.einsum("bmav,wmv->mabw", qmat, kmat, preferred_element_type=jnp.float32) * scale
    scores = jnp.where(same[None, None], scores, -1e30)
    probs = jax.nn.softmax(scores, axis=-1)
    probs_half = probs.astype(jnp.bfloat16)
    value_gradient = jnp.einsum(
        "kgtu,tkgd->ukd", probs_half, output_matrix, preferred_element_type=jnp.float32
    ).astype(jnp.bfloat16)
    probability_grad = jnp.einsum(
        "bmav,wmv->mabw", output_matrix, value_matrix, preferred_element_type=jnp.float32
    )
    row_dots = jnp.sum(probs * probability_grad, axis=-1, keepdims=True)
    score_grad = (probs * (probability_grad - row_dots) * scale).astype(jnp.bfloat16)
    query_gradient = jnp.einsum(
        "kgtu,ukd->tkgd", score_grad, kmat, preferred_element_type=jnp.float32
    ).astype(jnp.bfloat16)
    key_gradient = jnp.einsum(
        "kgtu,tkgd->ukd", score_grad, qmat, preferred_element_type=jnp.float32
    ).astype(jnp.bfloat16)
    return (
        query_gradient.reshape(token_count, -1),
        key_gradient.reshape(token_count, -1),
        value_gradient.reshape(token_count, -1),
    )


def rows_product(left, piece):
    return lax.dot_general(
        left, piece, (((1,), (1,)), ((), ())), preferred_element_type=jnp.float32
    )


def adapter_total(
    normed, adapter_middle, middle_gradient, query_gradient, key_gradient, value_gradient
):
    down_local = lax.dot_general(
        normed, middle_gradient, (((0,), (0,)), ((), ())), preferred_element_type=jnp.float32
    )
    local_query = adapter_scale * lax.dot_general(
        adapter_middle[:, 0:ADAPTER_RANK],
        query_gradient,
        (((0,), (0,)), ((), ())),
        preferred_element_type=jnp.float32,
    )
    local_key = adapter_scale * lax.dot_general(
        adapter_middle[:, ADAPTER_RANK : 2 * ADAPTER_RANK],
        key_gradient,
        (((0,), (0,)), ((), ())),
        preferred_element_type=jnp.float32,
    )
    local_value = adapter_scale * lax.dot_general(
        adapter_middle[:, 2 * ADAPTER_RANK : 3 * ADAPTER_RANK],
        value_gradient,
        (((0,), (0,)), ((), ())),
        preferred_element_type=jnp.float32,
    )
    down_total, query_total, key_value_total = lax.psum(
        (down_local, local_query, jnp.stack([local_key, local_value])), "dp"
    )
    return (down_total, query_total, key_value_total)


def shards(
    normed,
    stored_queries,
    stored_keys,
    stored_values,
    head_output_grad,
    document_index,
    query_projection_weight,
    key_projection_weight,
    value_projection_weight,
    adapter_down_maps,
    query_up_map,
    key_value_up_maps,
):
    query_gradient, key_gradient, value_gradient = attention_backward(
        stored_queries, stored_keys, stored_values, head_output_grad, document_index[0]
    )
    local_middle = jnp.dot(normed, adapter_down_maps, preferred_element_type=jnp.float32)
    grad_local = jnp.concatenate(
        [
            adapter_scale * rows_product(query_gradient, query_up_map),
            adapter_scale * rows_product(key_gradient, key_value_up_maps[0]),
            adapter_scale * rows_product(value_gradient, key_value_up_maps[1]),
        ],
        axis=1,
    )
    middle_total, grad_sum = (
        lax.psum(local_middle.astype(jnp.bfloat16), "tensor").astype(jnp.float32),
        lax.psum(grad_local.astype(jnp.bfloat16), "tensor").astype(jnp.float32),
    )
    adapter_middle = middle_total.astype(jnp.bfloat16)
    middle_gradient = grad_sum.astype(jnp.bfloat16)
    base_term = rows_product(
        query_gradient, lax.all_gather(query_projection_weight, "dp", axis=0, tiled=True)
    )
    base_term = base_term + rows_product(
        key_gradient, lax.all_gather(key_projection_weight, "dp", axis=0, tiled=True)
    )
    base_term = base_term + rows_product(
        value_gradient, lax.all_gather(value_projection_weight, "dp", axis=0, tiled=True)
    )
    base_offset = lax.psum_scatter(
        base_term.astype(jnp.bfloat16), "tensor", scatter_dimension=1, tiled=True
    ).astype(jnp.float32)
    normed_input_grad = (
        base_offset
        + lax.dot_general(
            middle_gradient,
            adapter_down_maps,
            (((1,), (1,)), ((), ())),
            preferred_element_type=jnp.float32,
        )
    ).astype(jnp.bfloat16)
    down_total, query_total, key_value_total = adapter_total(
        normed, adapter_middle, middle_gradient, query_gradient, key_gradient, value_gradient
    )
    return (normed_input_grad, down_total, query_total, key_value_total)


def solution(mesh):
    in_specs = (
        P("dp", "tensor"),
        P("dp", "tensor"),
        P("dp", "tensor"),
        P("dp", "tensor"),
        P("dp", "tensor"),
        P("dp", None),
        P("dp", "tensor"),
        P("dp", "tensor"),
        P("dp", "tensor"),
        P("tensor", None),
        P(None, "tensor"),
        P(None, None, "tensor"),
    )
    out_specs = (P("dp", "tensor"), P("tensor", None), P(None, "tensor"), P(None, None, "tensor"))
    return jax.shard_map(shards, mesh=mesh, in_specs=in_specs, out_specs=out_specs, check_vma=False)
```

profile of v0, /device:TPU:0, one launch (start us, length us, event | category | flops | bytes accessed | tf_op | source)
XLA Modules:
  0.0 785.0 jit_solution(11246477289122399510)
XLA Ops:
  10.9 2.6 reshape.63
  13.6 1.2 reshape.64
  15.5 2.2 fusion.34
  17.7 2.6 fusion.67
  20.3 7.6 fusion.15
  29.2 6.3 fusion.24
  35.5 2.7 fusion.25
  39.6 1.2 convolution_convert_fusion.1
  41.1 324.1 %all-gather.4.cloned.1.call-done = bf16[8192,2048]{1,0:T(8,128)(2,1)} async-done(((bf16[512,2048]{1,0:T(8,128)(2,1)}), bf16[8192,2048]{1,0:T(8,128)(2,1)}) %all-gather.4.cloned.1.call-update) | async-done | bytes 33554448 | tf_op jit(solution)/shard_map/all_gather | solution.py:118
  365.2 18.4 %fusion.68 = f32[192,8192]{1,0:T(8,128)} fusion(bf16[192,2048]{1,0:T(8,128)(2,1)S(1)} %reshape.66, bf16[8192,2048]{1,0:T(8,128)(2,1)} %all-gather.4.cloned.1.call-done), kind=kOutput, calls=%fused_computation.82 | convolution fusion | flops 6442450944 | bytes 40632320 | tf_op jit(solution)/shard_map/dot_general | solution.py:50
  383.6 95.4 %all-gather.6.cloned.1.call-done = bf16[8192,512]{1,0:T(8,128)(2,1)} async-done(((bf16[512,512]{1,0:T(8,128)(2,1)}), bf16[8192,512]{1,0:T(8,128)(2,1)}) %all-gather.6.cloned.1.call-update) | async-done | bytes 8388624 | tf_op jit(solution)/shard_map/all_gather | solution.py:121
  479.1 10.6 %convolution_add_fusion.1 = f32[192,8192]{1,0:T(8,128)} fusion(f32[192,8192]{1,0:T(8,128)} %fusion.68, bf16[8192,512]{1,0:T(8,128)(2,1)} %all-gather.6.cloned.1.call-done, bf16[4,24,8,128]{3,2,1,0:T(8,128)(2,1)S(1)} %fusion.24), kind=kOutput, calls=%fused_computation.3 | convolution fusion | flops 1612185600 | bytes 21168128 | tf_op jit(solution)/shard_map/dot_general | solution.py:50
  489.7 103.2 %all-gather.8.cloned.1.call-done = bf16[8192,512]{1,0:T(8,128)(2,1)} async-done(((bf16[512,512]{1,0:T(8,128)(2,1)}), bf16[8192,512]{1,0:T(8,128)(2,1)}) %all-gather.8.cloned.1.call-update) | async-done | bytes 8388624 | tf_op jit(solution)/shard_map/all_gather | solution.py:124
  592.9 9.7 %fusion.2 = bf16[192,8192]{1,0:T(8,128)(2,1)} fusion(f32[192,8192]{1,0:T(8,128)} %convolution_add_fusion.1, bf16[8192,512]{1,0:T(8,128)(2,1)} %all-gather.8.cloned.1.call-done, bf16[4,24,8,128]{3,2,1,0:T(8,128)(2,1)S(1)} %fusion.25), kind=kOutput, calls=%fused_computation.4 | convolution fusion | flops 1613758464 | bytes 18022400 | tf_op jit(solution)/shard_map/dot_general | solution.py:50
  602.7 1.0 fusion.28
  603.7 1.1 fusion.29
  604.8 0.7 pad_maximum_fusion
  605.5 1.9 convolution_multiply_fusion
  607.4 3.1 convolution_bitcast_fusion
  610.5 1.1 reduce-scatter.2.cloned.1.call-done
  612.0 3.2 fusion.3
  615.2 157.2 %all-reduce.5.cloned.1.call-done = (f32[4096,192]{0,1:T(8,128)}, f32[64,2048]{1,0:T(8,128)}, f32[2,64,512]{2,1,0:T(8,128)}) async-done(((f32[4096,192]{0,1:T(8,128)}, f32[64,2048]{1,0:T(8,128)}, f32[2,64,512]{2,1,0:T(8,128)}), (f32[4096,192]{0,1:T(8,128)}, f32[64,2048]{1,0:T(8,128)}, f32[2,64,512]{2,1,0:T(8,128)})) %all-reduce.5.cloned.1.call-update) | async-done | bytes 3932176 | tf_op jit(solution)/shard_map/psum | solution.py:79
  772.4 3.9 copy.92
  776.4 0.8 copy.93
  (52 shorter events, 7.6 us)
Async XLA Ops:
  8.0 31.6 %copy-start = (bf16[192,4096]{1,0:T(8,128)(2,1)S(1)}, bf16[192,4096]{1,0:T(8,128)(2,1)}, u32[]{:S(2)}) copy-start(bf16[192,4096]{1,0:T(8,128)(2,1)} %param.12) | copy-start | bytes 4718596
  8.0 2.3 copy-start.6
  8.0 5.5 copy-start.11
  8.0 6.7 copy-start.12
  8.0 357.2 %all-gather.4.cloned.1.call-start = ((), (), s32[]{:S(2)}) async-start(), calls=%async_computation.1 | async-start | bytes 35651584 | tf_op jit(solution)/shard_map/all_gather | solution.py:118
  8.8 470.3 %all-gather.6.cloned.1.call-start = ((), (), s32[]{:S(2)}) async-start(), calls=%async_computation.2 | async-start | bytes 8912896 | tf_op jit(solution)/shard_map/all_gather | solution.py:121
  9.5 583.4 %all-gather.8.cloned.1.call-start = ((), (), s32[]{:S(2)}) async-start(), calls=%async_computation.3 | async-start | bytes 8912896 | tf_op jit(solution)/shard_map/all_gather | solution.py:124
  10.3 592.4 %all-reduce.7.cloned.1.call-start = ((), (), s32[]{:S(2)}) async-start(), calls=%async_computation.6 | async-start | bytes 393216 | tf_op jit(solution)/shard_map/psum | solution.py:113
  10.9 4.6 copy-start.1
  13.5 4.2 copy-start.3
  29.1 6.3 copy-start.2
  35.4 2.7 copy-start.13
  35.5 3.1 copy-start.10
  35.5 4.1 copy-start.4
  40.9 570.8 %reduce-scatter.2.cloned.1.call-start = ((), (), s32[]{:S(2)}) async-start(), calls=%async_computation.4 | async-start | bytes 4718592 | tf_op jit(solution)/shard_map/reduce_scatter | solution.py:126
  602.6 169.8 %all-reduce.5.cloned.1.call-start = ((), (), s32[]{:S(2)}) async-start(), calls=%async_computation.5 | async-start | bytes 7864320 | tf_op jit(solution)/shard_map/psum | solution.py:79
  610.5 1.5 copy-start.5
  610.5 1.5 copy-start.8
  772.4 3.9 copy-start.7
  772.4 4.7 copy-start.9
Sparse Core Ops, SparseCore 0:
  11.7 353.5 all-gather.3
  368.0 111.0 all-gather.5
  481.8 111.0 all-gather.7
  610.9 161.4 all-reduce.4
Sparse Core Ops, SparseCore 1:
  41.0 20.6 all-reduce.6
  602.7 8.9 reduce-scatter.1
where the time goes:
time: 785 us
  waiting for transfers between devices  683 us (87%)
  matrix products  70.3 us (9%)
  between operations  15.4 us (2%)
  local copies, waits for them, and re-layouts  11.5 us (1%)
    all_gather x1, waiting for transfers between devices, shards(): lax.all_gather(query_projection_weight, 'dp', axis=0, tiled=True)  324 us
    psum x1, waiting for transfers between devices, adapter_total(): lax.psum((down_local, local_query, jnp.stack([local_key, local_value])),...  157 us
    all_gather x1, waiting for transfers between devices, shards(): lax.all_gather(value_projection_weight, 'dp', axis=0, tiled=True)  103 us
    all_gather x1, waiting for transfers between devices, shards(): lax.all_gather(key_projection_weight, 'dp', axis=0, tiled=True)  95.4 us
    dot_general x6, matrix products, rows_product(): lax.dot_general(left, piece, (((1,), (1,)), ((), ())), preferred_element_...  39.5 us
  transfers between devices with their start and end apart: 6, of which 5 were waited for; matrix products, arithmetic and copies ran while one was open for 10% of the time, Pallas kernels for 0%

commit v1 on v0

--- a/solution.py
+++ b/solution.py
@@ -9,6 +9,19 @@
 HEAD_SIZE = 128
 ADAPTER_RANK = 64
 adapter_scale = 0.5
+
+
+def ring_gather(x, axis, dim):
+    ways = lax.axis_size(axis)
+    up = [(d, (d + 1) % ways) for d in range(ways)]
+    down = [(d, (d - 1) % ways) for d in range(ways)]
+    earlier, later = ([x], [x])
+    for _ in range(ways // 2):
+        earlier.append(lax.ppermute(earlier[-1], axis, up))
+    for _ in range((ways - 1) // 2):
+        later.append(lax.ppermute(later[-1], axis, down))
+    line = jnp.concatenate([*earlier[::-1], *later[1:]], axis=dim)
+    return jnp.roll(line, (lax.axis_index(axis) - ways // 2) * x.shape[dim], axis=dim)
 
 
 def attention_backward(queries, keyrows, value_row_block, output_gradient, ids):
@@ -114,9 +127,7 @@
     )
     adapter_middle = middle_total.astype(jnp.bfloat16)
     middle_gradient = grad_sum.astype(jnp.bfloat16)
-    base_term = rows_product(
-        query_gradient, lax.all_gather(query_projection_weight, "dp", axis=0, tiled=True)
-    )
+    base_term = rows_product(query_gradient, ring_gather(query_projection_weight, "dp", 0))
     base_term = base_term + rows_product(
         key_gradient, lax.all_gather(key_projection_weight, "dp", axis=0, tiled=True)
     )

time: 785 us -> 1100 us (1.40)
  waiting for transfers between devices: 683 us -> 850 us
  local copies, waits for them, and re-layouts: 11.5 us -> 98.8 us
  starting transfers between devices: 0.42 us -> 59 us
    ppermute x0 -> x15, waiting for transfers between devices: none -> 684 us  [the longest x8 684 us: ring_gather(): earlier.append(lax.ppermute(earlier[-1], axis, up))]
    all_gather x1 -> x0, waiting for transfers between devices: 324 us -> none  [shards(): lax.all_gather(query_projection_weight, 'dp', axis=0, tiled=True)]
    all_gather x1, waiting for transfers between devices: 103 us -> 0.01 us  [shards(): lax.all_gather(value_projection_weight, 'dp', axis=0, tiled=True)]
    all_gather x1, waiting for transfers between devices: 95.4 us -> 0.01 us  [shards(): lax.all_gather(key_projection_weight, 'dp', axis=0, tiled=True)]
    unnamed x31 -> x90, local copies, waits for them, and re-layouts: 5.85 us -> 87.5 us
    ppermute x0 -> x15, starting transfers between devices: none -> 58.7 us  [the longest x7 40.8 us: ring_gather(): later.append(lax.ppermute(later[-1], axis, down))]
  transfers between devices with their start and end apart: 6 -> 20, of which waited for: 5 -> 10; matrix products, arithmetic and copies ran while one was open for 10% -> 15% of each run, Pallas kernels for 0% -> 0%
where the time goes in v1:
time: 1100 us
  waiting for transfers between devices  850 us (77%)
  local copies, waits for them, and re-layouts  98.8 us (9%)
  matrix products  68.8 us (6%)
  starting transfers between devices  59 us (5%)
  between operations  15.5 us (1%)
    ppermute x8, waiting for transfers between devices, ring_gather(): earlier.append(lax.ppermute(earlier[-1], axis, up))  684 us
    psum x1, waiting for transfers between devices, adapter_total(): lax.psum((down_local, local_query, jnp.stack([local_key, local_value])),...  157 us
    unnamed x90, local copies, waits for them, and re-layouts  87.5 us
    ppermute x7, starting transfers between devices, ring_gather(): later.append(lax.ppermute(later[-1], axis, down))  40.8 us
    dot_general x6, matrix products, rows_product(): lax.dot_general(left, piece, (((1,), (1,)), ((), ())), preferred_element_...  40.4 us
  transfers between devices with their start and end apart: 20, of which 10 were waited for; matrix products, arithmetic and copies ran while one was open for 15% of the time, Pallas kernels for 0%

profile of v1, /device:TPU:0, one launch (start us, length us, event | category | flops | bytes accessed | tf_op | source)
XLA Modules:
  0.0 1099.8 jit_solution(2152764267661387155)
XLA Ops:
  12.5 75.2 %collective-permute-done = bf16[512,2048]{1,0:T(8,128)(2,1)S(1)} collective-permute-done((bf16[512,2048]{1,0:T(8,128)(2,1)}, bf16[512,2048]{1,0:T(8,128)(2,1)S(1)}, u32[]{:S(2)}, u32[]{:S(2)}) %collective-permute-start) | collective-permute-done | bytes 2097184 | tf_op jit(solution)/shard_map/ppermute | solution.py:20
  89.1 5.6 collective-permute-start.8
  94.7 112.6 %collective-permute-done.1 = bf16[512,2048]{1,0:T(8,128)(2,1)S(1)} collective-permute-done((bf16[512,2048]{1,0:T(8,128)(2,1)S(1)}, bf16[512,2048]{1,0:T(8,128)(2,1)S(1)}, u32[]{:S(2)}, u32[]{:S(2)}) %collective-permute-start.1) | collective-permute-done | bytes 2097184 | tf_op jit(solution)/shard_map/ppermute | solution.py:20
  211.1 5.4 collective-permute-start.9
  216.4 99.1 %collective-permute-done.2 = bf16[512,2048]{1,0:T(8,128)(2,1)S(1)} collective-permute-done((bf16[512,2048]{1,0:T(8,128)(2,1)S(1)}, bf16[512,2048]{1,0:T(8,128)(2,1)S(1)}, u32[]{:S(2)}, u32[]{:S(2)}) %collective-permute-start.2) | collective-permute-done | bytes 2097184 | tf_op jit(solution)/shard_map/ppermute | solution.py:20
  318.1 7.9 collective-permute-start.10
  326.0 111.5 %collective-permute-done.3 = bf16[512,2048]{1,0:T(8,128)(2,1)S(1)} collective-permute-done((bf16[512,2048]{1,0:T(8,128)(2,1)S(1)}, bf16[512,2048]{1,0:T(8,128)(2,1)S(1)}, u32[]{:S(2)}, u32[]{:S(2)}) %collective-permute-start.3) | collective-permute-done | bytes 2097184 | tf_op jit(solution)/shard_map/ppermute | solution.py:20
  440.0 7.0 collective-permute-start.11
  447.0 82.1 %collective-permute-done.4 = bf16[512,2048]{1,0:T(8,128)(2,1)} collective-permute-done((bf16[512,2048]{1,0:T(8,128)(2,1)S(1)}, bf16[512,2048]{1,0:T(8,128)(2,1)}, u32[]{:S(2)}, u32[]{:S(2)}) %collective-permute-start.4) | collective-permute-done | bytes 2097184 | tf_op jit(solution)/shard_map/ppermute | solution.py:20
  531.7 5.7 collective-permute-start.12
  545.0 74.5 %collective-permute-done.5 = bf16[512,2048]{1,0:T(8,128)(2,1)} collective-permute-done((bf16[512,2048]{1,0:T(8,128)(2,1)}, bf16[512,2048]{1,0:T(8,128)(2,1)}, u32[]{:S(2)}, u32[]{:S(2)}) %collective-permute-start.5) | collective-permute-done | bytes 2097184 | tf_op jit(solution)/shard_map/ppermute | solution.py:20
  630.1 6.0 fusion.24
  637.3 6.2 fusion.33
  646.5 65.8 %collective-permute-done.6 = bf16[512,2048]{1,0:T(8,128)(2,1)} collective-permute-done((bf16[512,2048]{1,0:T(8,128)(2,1)}, bf16[512,2048]{1,0:T(8,128)(2,1)}, u32[]{:S(2)}, u32[]{:S(2)}) %collective-permute-start.6) | collective-permute-done | bytes 2097184 | tf_op jit(solution)/shard_map/ppermute | solution.py:20
  717.4 6.0 collective-permute-start.14
  723.4 8.9 fusion.54
  732.3 8.9 fusion.50
  741.2 63.0 %collective-permute-done.7 = bf16[512,2048]{1,0:T(8,128)(2,1)} collective-permute-done((bf16[512,2048]{1,0:T(8,128)(2,1)}, bf16[512,2048]{1,0:T(8,128)(2,1)}, u32[]{:S(2)}, u32[]{:S(2)}) %collective-permute-start.7) | collective-permute-done | bytes 2097184 | tf_op jit(solution)/shard_map/ppermute | solution.py:20
  813.9 3.4 constant_dynamic-update-slice_fusion.28
  885.4 21.9 %fusion.10 = bf16[192,8192]{1,0:T(8,128)(2,1)} fusion(f32[192,8192]{1,0:T(8,128)} %fusion.50, f32[192,8192]{1,0:T(8,128)} %fusion.54, bf16[192,2048]{1,0:T(8,128)(2,1)S(1)} %reshape.66, bf16[16384,2048]{1,0:T(8,128)(2,1)} %constant_dynamic-update-slice_fusion, s32[]{:T(128)S(6)} %select_n.19), kind=kOutput, calls=%fused_computation.6 | convolution fusion | flops 6447169536 | bytes 50069508 | tf_op jit(solution)/shard_map/dot_general | solution.py:63
  918.9 7.3 reduce-scatter.2.cloned.1.call-done
  926.2 3.9 add_convert_fusion
  930.0 157.2 %all-reduce.5.cloned.1.call-done = (f32[4096,192]{0,1:T(8,128)}, f32[64,2048]{1,0:T(8,128)}, f32[2,64,512]{2,1,0:T(8,128)}) async-done(((f32[4096,192]{0,1:T(8,128)}, f32[64,2048]{1,0:T(8,128)}, f32[2,64,512]{2,1,0:T(8,128)}), (f32[4096,192]{0,1:T(8,128)}, f32[64,2048]{1,0:T(8,128)}, f32[2,64,512]{2,1,0:T(8,128)})) %all-reduce.5.cloned.1.call-update) | async-done | bytes 3932176 | tf_op jit(solution)/shard_map/psum | solution.py:92
  1087.3 3.9 copy.123
  (140 shorter events, 135.2 us)
Async XLA Ops:
  8.0 708.0 %copy-start = (bf16[192,4096]{1,0:T(8,128)(2,1)S(1)}, bf16[192,4096]{1,0:T(8,128)(2,1)}, u32[]{:S(2)}) copy-start(bf16[192,4096]{1,0:T(8,128)(2,1)} %param.12) | copy-start | bytes 4718596
  8.0 715.4 %all-gather.3.cloned.1.call-start = ((), (), s32[]{:S(2)}) async-start(), calls=%async_computation.1 | async-start | bytes 8912896 | tf_op jit(solution)/shard_map/all_gather | solution.py:132
  8.7 723.6 %all-gather.5.cloned.1.call-start = ((), (), s32[]{:S(2)}) async-start(), calls=%async_computation.2 | async-start | bytes 8912896 | tf_op jit(solution)/shard_map/all_gather | solution.py:135
  9.5 897.9 %all-reduce.7.cloned.1.call-start = ((), (), s32[]{:S(2)}) async-start(), calls=%async_computation.5 | async-start | bytes 393216 | tf_op jit(solution)/shard_map/psum | solution.py:126
  9.5 78.2 %collective-permute-start = (bf16[512,2048]{1,0:T(8,128)(2,1)}, bf16[512,2048]{1,0:T(8,128)(2,1)S(1)}, u32[]{:S(2)}, u32[]{:S(2)}) collective-permute-start(bf16[512,2048]{1,0:T(8,128)(2,1)} %param.18), channel_id=1, source_target_pairs={{0,2},{2,4},{4,6},{6,8},{8,10},{10,12},{12,14},{14,16},{16,18},{18... | collective-permute-start | bytes 6291464 | tf_op jit(solution)/shard_map/ppermute | solution.py:20
  89.1 118.2 %collective-permute-start.1 = (bf16[512,2048]{1,0:T(8,128)(2,1)S(1)}, bf16[512,2048]{1,0:T(8,128)(2,1)S(1)}, u32[]{:S(2)}, u32[]{:S(2)}) collective-permute-start(bf16[512,2048]{1,0:T(8,128)(2,1)S(1)} %collective-permute-done), channel_id=1, source_target_pairs={{0,2},{2,4},{4,6},{6,8},{8,10},{10,12},{12,14},{14,16},{16,18},{18... | collective-permute-start | bytes 6291464 | tf_op jit(solution)/shard_map/ppermute | solution.py:20
  89.1 120.7 %collective-permute-start.8 = (bf16[512,2048]{1,0:T(8,128)(2,1)}, bf16[512,2048]{1,0:T(8,128)(2,1)S(1)}, u32[]{:S(2)}, u32[]{:S(2)}) collective-permute-start(bf16[512,2048]{1,0:T(8,128)(2,1)} %param.18), channel_id=1, source_target_pairs={{0,30},{2,0},{4,2},{6,4},{8,6},{10,8},{12,10},{14,12},{16,14},{18,... | collective-permute-start | bytes 6291464 | tf_op jit(solution)/shard_map/ppermute | solution.py:22
  207.3 110.8 %copy-start.6 = (bf16[512,2048]{1,0:T(8,128)(2,1)}, bf16[512,2048]{1,0:T(8,128)(2,1)S(1)}, u32[]{:S(2)}) copy-start(bf16[512,2048]{1,0:T(8,128)(2,1)S(1)} %collective-permute-done.1) | copy-start | bytes 6291460
  207.3 108.3 %collective-permute-start.2 = (bf16[512,2048]{1,0:T(8,128)(2,1)S(1)}, bf16[512,2048]{1,0:T(8,128)(2,1)S(1)}, u32[]{:S(2)}, u32[]{:S(2)}) collective-permute-start(bf16[512,2048]{1,0:T(8,128)(2,1)S(1)} %collective-permute-done.1), channel_id=1, source_target_pairs={{0,2},{2,4},{4,6},{6,8},{8,10},{10,12},{12,14},{14,16},{16,18},{18... | collective-permute-start | bytes 6291464 | tf_op jit(solution)/shard_map/ppermute | solution.py:20
  211.1 107.0 %collective-permute-start.9 = (bf16[512,2048]{1,0:T(8,128)(2,1)S(1)}, bf16[512,2048]{1,0:T(8,128)(2,1)S(1)}, u32[]{:S(2)}, u32[]{:S(2)}) collective-permute-start(bf16[512,2048]{1,0:T(8,128)(2,1)S(1)} %collective-permute-done.8), channel_id=1, source_target_pairs={{0,30},{2,0},{4,2},{6,4},{8,6},{10,8},{12,10},{14,12},{16,14},{18,... | collective-permute-start | bytes 6291464 | tf_op jit(solution)/shard_map/ppermute | solution.py:22
  315.6 124.4 %copy-start.10 = (bf16[512,2048]{1,0:T(8,128)(2,1)}, bf16[512,2048]{1,0:T(8,128)(2,1)S(1)}, u32[]{:S(2)}) copy-start(bf16[512,2048]{1,0:T(8,128)(2,1)S(1)} %collective-permute-done.2) | copy-start | bytes 6291460
  315.6 121.9 %collective-permute-start.3 = (bf16[512,2048]{1,0:T(8,128)(2,1)S(1)}, bf16[512,2048]{1,0:T(8,128)(2,1)S(1)}, u32[]{:S(2)}, u32[]{:S(2)}) collective-permute-start(bf16[512,2048]{1,0:T(8,128)(2,1)S(1)} %collective-permute-done.2), channel_id=1, source_target_pairs={{0,2},{2,4},{4,6},{6,8},{8,10},{10,12},{12,14},{14,16},{16,18},{18... | collective-permute-start | bytes 6291464 | tf_op jit(solution)/shard_map/ppermute | solution.py:20
  318.1 121.9 %collective-permute-start.10 = (bf16[512,2048]{1,0:T(8,128)(2,1)S(1)}, bf16[512,2048]{1,0:T(8,128)(2,1)S(1)}, u32[]{:S(2)}, u32[]{:S(2)}) collective-permute-start(bf16[512,2048]{1,0:T(8,128)(2,1)S(1)} %collective-permute-done.9), channel_id=1, source_target_pairs={{0,30},{2,0},{4,2},{6,4},{8,6},{10,8},{12,10},{14,12},{16,14},{18,... | collective-permute-start | bytes 6291464 | tf_op jit(solution)/shard_map/ppermute | solution.py:22
  437.5 94.2 %copy-start.14 = (bf16[512,2048]{1,0:T(8,128)(2,1)}, bf16[512,2048]{1,0:T(8,128)(2,1)S(1)}, u32[]{:S(2)}) copy-start(bf16[512,2048]{1,0:T(8,128)(2,1)S(1)} %collective-permute-done.3) | copy-start | bytes 6291460
  437.5 91.6 %collective-permute-start.4 = (bf16[512,2048]{1,0:T(8,128)(2,1)S(1)}, bf16[512,2048]{1,0:T(8,128)(2,1)}, u32[]{:S(2)}, u32[]{:S(2)}) collective-permute-start(bf16[512,2048]{1,0:T(8,128)(2,1)S(1)} %collective-permute-done.3), channel_id=1, source_target_pairs={{0,2},{2,4},{4,6},{6,8},{8,10},{10,12},{12,14},{14,16},{16,18},{18... | collective-permute-start | bytes 6291464 | tf_op jit(solution)/shard_map/ppermute | solution.py:20
  440.0 91.7 %collective-permute-start.11 = (bf16[512,2048]{1,0:T(8,128)(2,1)S(1)}, bf16[512,2048]{1,0:T(8,128)(2,1)}, u32[]{:S(2)}, u32[]{:S(2)}) collective-permute-start(bf16[512,2048]{1,0:T(8,128)(2,1)S(1)} %collective-permute-done.10), channel_id=1, source_target_pairs={{0,30},{2,0},{4,2},{6,4},{8,6},{10,8},{12,10},{14,12},{16,14},{18,... | collective-permute-start | bytes 6291464 | tf_op jit(solution)/shard_map/ppermute | solution.py:22
  529.1 90.4 %collective-permute-start.5 = (bf16[512,2048]{1,0:T(8,128)(2,1)}, bf16[512,2048]{1,0:T(8,128)(2,1)}, u32[]{:S(2)}, u32[]{:S(2)}) collective-permute-start(bf16[512,2048]{1,0:T(8,128)(2,1)} %collective-permute-done.4), channel_id=1, source_target_pairs={{0,2},{2,4},{4,6},{6,8},{8,10},{10,12},{12,14},{14,16},{16,18},{18... | collective-permute-start | bytes 6291464 | tf_op jit(solution)/shard_map/ppermute | solution.py:20
  531.7 95.3 %collective-permute-start.12 = (bf16[512,2048]{1,0:T(8,128)(2,1)}, bf16[512,2048]{1,0:T(8,128)(2,1)}, u32[]{:S(2)}, u32[]{:S(2)}) collective-permute-start(bf16[512,2048]{1,0:T(8,128)(2,1)} %collective-permute-done.11), channel_id=1, source_target_pairs={{0,30},{2,0},{4,2},{6,4},{8,6},{10,8},{12,10},{14,12},{16,14},{18,... | collective-permute-start | bytes 6291464 | tf_op jit(solution)/shard_map/ppermute | solution.py:22
  619.5 92.8 %collective-permute-start.6 = (bf16[512,2048]{1,0:T(8,128)(2,1)}, bf16[512,2048]{1,0:T(8,128)(2,1)}, u32[]{:S(2)}, u32[]{:S(2)}) collective-permute-start(bf16[512,2048]{1,0:T(8,128)(2,1)} %collective-permute-done.5), channel_id=1, source_target_pairs={{0,2},{2,4},{4,6},{6,8},{8,10},{10,12},{12,14},{14,16},{16,18},{18... | collective-permute-start | bytes 6291464 | tf_op jit(solution)/shard_map/ppermute | solution.py:20
  627.0 90.4 %collective-permute-start.13 = (bf16[512,2048]{1,0:T(8,128)(2,1)}, bf16[512,2048]{1,0:T(8,128)(2,1)}, u32[]{:S(2)}, u32[]{:S(2)}) collective-permute-start(bf16[512,2048]{1,0:T(8,128)(2,1)} %collective-permute-done.12), channel_id=1, source_target_pairs={{0,30},{2,0},{4,2},{6,4},{8,6},{10,8},{12,10},{14,12},{16,14},{18,... | collective-permute-start | bytes 6291464 | tf_op jit(solution)/shard_map/ppermute | solution.py:22
  712.3 92.0 %collective-permute-start.7 = (bf16[512,2048]{1,0:T(8,128)(2,1)}, bf16[512,2048]{1,0:T(8,128)(2,1)}, u32[]{:S(2)}, u32[]{:S(2)}) collective-permute-start(bf16[512,2048]{1,0:T(8,128)(2,1)} %collective-permute-done.6), channel_id=1, source_target_pairs={{0,2},{2,4},{4,6},{6,8},{8,10},{10,12},{12,14},{14,16},{16,18},{18... | collective-permute-start | bytes 6291464 | tf_op jit(solution)/shard_map/ppermute | solution.py:20
  717.3 208.9 %reduce-scatter.2.cloned.1.call-start = ((), (), s32[]{:S(2)}) async-start(), calls=%async_computation.3 | async-start | bytes 4718592 | tf_op jit(solution)/shard_map/reduce_scatter | solution.py:137
  717.4 127.4 %collective-permute-start.14 = (bf16[512,2048]{1,0:T(8,128)(2,1)}, bf16[512,2048]{1,0:T(8,128)(2,1)}, u32[]{:S(2)}, u32[]{:S(2)}) collective-permute-start(bf16[512,2048]{1,0:T(8,128)(2,1)} %collective-permute-done.13), channel_id=1, source_target_pairs={{0,30},{2,0},{4,2},{6,4},{8,6},{10,8},{12,10},{14,12},{16,14},{18,... | collective-permute-start | bytes 6291464 | tf_op jit(solution)/shard_map/ppermute | solution.py:22
  907.3 180.0 %all-reduce.5.cloned.1.call-start = ((), (), s32[]{:S(2)}) async-start(), calls=%async_computation.4 | async-start | bytes 7864320 | tf_op jit(solution)/shard_map/psum | solution.py:92
  (24 other events, 443.5 us)
Sparse Core Ops, SparseCore 0:
  11.6 185.5 all-gather.2
  200.0 248.4 all-gather.4
  915.9 171.3 all-reduce.4
Sparse Core Ops, SparseCore 1:
  717.4 71.8 all-reduce.6
  907.4 18.7 reduce-scatter.1
